TPU v7x, 32 devices: a whole 2x2x4 slice. The times are simulated.
32 devices in a mesh: rows: 8 (over y, x, core), tp: 4 (over z).
Axes of the slice: x: 2, y: 2, z: 4, core: 2. Of those that a mesh axis runs over, the one named last changes fastest.
Arguments:
- first_query: float32 [9216, 9216], P('rows', 'tp'), may hold values from -0.09375 to 0.09375
- second_query: float32 [9216, 9216], P('rows', 'tp'), may hold values from -0.0625 to 0.0625
- first_key: float32 [9216, 9216], P('rows', 'tp'), may hold values from -0.09375 to 0.09375
- second_key: float32 [9216, 9216], P('rows', 'tp'), may hold values from -0.0625 to 0.0625
- first_value: float32 [9216, 9216], P('rows', 'tp'), may hold values from -0.09375 to 0.09375
- second_value: float32 [9216, 9216], P('rows', 'tp'), may hold values from -0.0625 to 0.0625
- mix_share: float32 [9216], P('rows'), may hold values from 0.2 to 0.8
- norm_train: float32 [9216], P(('rows', 'tp')), may hold values from 0.25 to 1.75
- norm_step: float32 [9216], P(('rows', 'tp')), may hold values from -0.3 to 0.3
Outputs:
- serving_query: bfloat16 [9216, 9216], P(None, ('tp', 'rows'))
- serving_key: bfloat16 [9216, 9216], P(None, ('tp', 'rows'))
- serving_value: bfloat16 [9216, 9216], P(None, ('tp', 'rows'))
- scale_query: float32 [9216], P(('tp', 'rows'))
- scale_key: float32 [9216], P(('tp', 'rows'))
- scale_value: float32 [9216], P(('tp', 'rows'))
- serve_norm: bfloat16 [9216], replicated
All inputs are finite; a program needn't handle non-finite values.
Results may differ from a plain program's by a relative error of at most 0.001.
Values may be sent and summed in bfloat16 or wider, within the bound.
A program may use at most 192 MiB of HBM per device.

v0:
```python
import jax
import jax.numpy as jnp
from jax import lax
from jax.sharding import PartitionSpec as P


def per_device(
    first_query,
    second_query,
    first_key,
    second_key,
    first_value,
    second_value,
    mix_share,
    norm_train,
    norm_step,
):
    whole_query = mix_share[:, None] * first_query + (1.0 - mix_share[:, None]) * second_query
    whole_key = mix_share[:, None] * first_key + (1.0 - mix_share[:, None]) * second_key
    whole_value = mix_share[:, None] * first_value + (1.0 - mix_share[:, None]) * second_value
    scale_query, scale_key, scale_value = lax.pmax(
        (
            jnp.max(jnp.abs(whole_query), axis=0),
            jnp.max(jnp.abs(whole_key), axis=0),
            jnp.max(jnp.abs(whole_value), axis=0),
        ),
        "rows",
    )
    narrow_query, narrow_key, narrow_value = (
        (whole_query / scale_query).astype(jnp.bfloat16),
        (whole_key / scale_key).astype(jnp.bfloat16),
        (whole_value / scale_value).astype(jnp.bfloat16),
    )
    serving_query, serving_key, serving_value = (
        lax.all_to_all(narrow_query, "rows", split_axis=1, concat_axis=0, tiled=True),
        lax.all_to_all(narrow_key, "rows", split_axis=1, concat_axis=0, tiled=True),
        lax.all_to_all(narrow_value, "rows", split_axis=1, concat_axis=0, tiled=True),
    )
    place = lax.axis_index("rows")
    scale_query = lax.dynamic_slice_in_dim(
        scale_query, place * serving_query.shape[1], serving_query.shape[1]
    )
    scale_key = lax.dynamic_slice_in_dim(
        scale_key, place * serving_key.shape[1], serving_key.shape[1]
    )
    scale_value = lax.dynamic_slice_in_dim(
        scale_value, place * serving_value.shape[1], serving_value.shape[1]
    )
    serve_norm = lax.all_gather(
        (norm_train + norm_step).astype(jnp.bfloat16), ("rows", "tp"), axis=0, tiled=True
    )
    return (
        serving_query,
        serving_key,
        serving_value,
        scale_query,
        scale_key,
        scale_value,
        serve_norm,
    )


def solution(mesh):
    return jax.shard_map(
        per_device,
        mesh=mesh,
        in_specs=(
            P("rows", "tp"),
            P("rows", "tp"),
            P("rows", "tp"),
            P("rows", "tp"),
            P("rows", "tp"),
            P("rows", "tp"),
            P("rows"),
            P(("rows", "tp")),
            P(("rows", "tp")),
        ),
        out_specs=(
            P(None, ("tp", "rows")),
            P(None, ("tp", "rows")),
            P(None, ("tp", "rows")),
            P(("tp", "rows")),
            P(("tp", "rows")),
            P(("tp", "rows")),
            P(),
        ),
        check_vma=False,
    )
```

profile of v0, /device:TPU:0, one launch (start us, length us, event | category | flops | bytes accessed | tf_op | source)
XLA Modules:
  0.0 396.1 jit_solution(8847732719092262777)
XLA Ops:
  0.6 12.7 %copy.25 = f32[1152,2304]{0,1:T(8,128)} copy(f32[1152,2304]{1,0:T(8,128)} %param.9) | data formatting | bytes 21233664 | tf_op args[0]
  13.3 12.7 %copy.26 = f32[1152,2304]{0,1:T(8,128)} copy(f32[1152,2304]{1,0:T(8,128)} %param.10) | data formatting | bytes 21233664 | tf_op args[1]
  26.0 12.7 %copy.28 = f32[1152,2304]{0,1:T(8,128)} copy(f32[1152,2304]{1,0:T(8,128)} %param.11) | data formatting | bytes 21233664 | tf_op args[2]
  38.7 12.7 %copy.29 = f32[1152,2304]{0,1:T(8,128)} copy(f32[1152,2304]{1,0:T(8,128)} %param.12) | data formatting | bytes 21233664 | tf_op args[3]
  51.4 12.7 %copy.31 = f32[1152,2304]{0,1:T(8,128)} copy(f32[1152,2304]{1,0:T(8,128)} %param.13) | data formatting | bytes 21233664 | tf_op args[4]
  64.1 12.7 %copy.32 = f32[1152,2304]{0,1:T(8,128)} copy(f32[1152,2304]{1,0:T(8,128)} %param.14) | data formatting | bytes 21233664 | tf_op args[5]
  76.7 21.5 %abs_reduce_fusion = (f32[2304]{0:T(1024)S(1)}, f32[2304]{0:T(1024)S(1)}, f32[2304]{0:T(1024)S(1)}) fusion(f32[1152,2304]{0,1:T(8,128)} %copy.32, f32[1152]{0:T(1024)S(1)} %broadcast_subtract_fusion, f32[1152,2304]{0,1:T(8,128)} %copy.31, f32[1152]{0:T(1024)S(1)} %copy-done, f32[1152,2304]{0,1:T(8,128)} %copy.29, f32[1152,2304]{0,1:T(8,128)} %copy.28, ...), kind=kLoop, calls=%fused_computation.1 | loop fusion | flops 39806208 | bytes 63737856 | tf_op jit(solution)/shard_map/reduce_max | solution.py:25
  98.3 25.8 %all-reduce.1 = (f32[2304]{0:T(1024)S(1)}, f32[2304]{0:T(1024)S(1)}, f32[2304]{0:T(1024)S(1)}) all-reduce(f32[2304]{0:T(1024)S(1)} %get-tuple-element.9, f32[2304]{0:T(1024)S(1)} %get-tuple-element.8, f32[2304]{0:T(1024)S(1)} %get-tuple-element.7), channel_id=1, replica_groups=mesh['rows'=8,'tp'=4] {'rows'}, use_global_device_ids=true, to_apply=%region_1.0 | all-reduce | flops 6912 | bytes 55296 | tf_op jit(solution)/shard_map/pmax | solution.py:21
  124.1 27.4 %divide_convert_fusion = (bf16[1152,2304]{0,1:T(8,128)(2,1)}, bf16[1152,2304]{0,1:T(8,128)(2,1)}, bf16[1152,2304]{0,1:T(8,128)(2,1)}) fusion(f32[2304]{0:T(1024)S(1)} %get-tuple-element.12, f32[1152,2304]{0,1:T(8,128)} %copy.32, f32[1152]{0:T(1024)S(1)} %broadcast_subtract_fusion, f32[1152,2304]{0,1:T(8,128)} %copy.31, f32[1152]{0:T(1024)S(1)} %copy-done, ...), kind=kLoop, calls=%fused_computation | loop fusion | flops 39813120 | bytes 79663104 | tf_op jit(solution)/shard_map/convert_element_type | solution.py:32
  151.5 65.9 %all_to_all.57 = bf16[1152,8,288]{0,2,1:T(8,128)(2,1)} all-to-all(bf16[1152,8,288]{0,2,1:T(8,128)(2,1)} %bitcast.20), channel_id=1, replica_groups=mesh['rows'=8,'tp'=4] {'rows'}, dimensions={1} | all-to-all | bytes 10616832 | tf_op jit(solution)/shard_map/all_to_all | solution.py:37
  217.5 0.0 copy-start.2
  217.5 64.5 %all_to_all.58 = bf16[1152,8,288]{0,2,1:T(8,128)(2,1)} all-to-all(bf16[1152,8,288]{0,2,1:T(8,128)(2,1)S(1)} %bitcast.19), channel_id=1, replica_groups=mesh['rows'=8,'tp'=4] {'rows'}, dimensions={1} | all-to-all | bytes 10616832 | tf_op jit(solution)/shard_map/all_to_all | solution.py:35
  281.9 4.7 %all-to-all-start.1 = ((bf16[1152,8,288]{0,2,1:T(8,128)(2,1)}), bf16[1152,8,288]{0,2,1:T(8,128)(2,1)}, u32[]{:S(2)}, u32[]{:S(2)}) async-start(bf16[1152,8,288]{0,2,1:T(8,128)(2,1)} %bitcast.16), calls=%async_computation.1 | async-start | bytes 10616832 | tf_op jit(solution)/shard_map/all_to_all | solution.py:36
  286.6 0.0 slice-start
  286.6 0.7 dynamic_slice.10
  287.3 0.7 dynamic_slice.11
  287.9 0.7 dynamic_slice.9
  288.6 0.0 copy-done.1
  288.6 0.3 dynamic-update-slice
  288.8 92.5 %all-reduce = bf16[9216]{0:T(1024)(128)(2,1)} all-reduce(bf16[9216]{0:T(1024)(128)(2,1)S(1)} %dynamic-update-slice), channel_id=1, replica_groups=mesh['rows'=8,'tp'=4] {'rows','tp'}, use_global_device_ids=true, to_apply=%add | all-reduce | flops 9216 | bytes 36864
  381.3 5.9 %copy.36 = bf16[8,36,8,1152]{3,2,0,1:T(8,128)(2,1)} copy(bf16[8,36,8,1152]{3,2,1,0:T(8,128)(2,1)} %bitcast.12) | data formatting | bytes 10616832 | tf_op jit(solution)/shard_map/all_to_all | solution.py:37
  387.2 3.2 copy.34
  390.4 0.0 all-to-all-done.1
  390.4 5.7 %copy.35 = bf16[8,36,8,1152]{3,2,0,1:T(8,128)(2,1)} copy(bf16[8,36,8,1152]{3,2,1,0:T(8,128)(2,1)} %bitcast.8) | data formatting | bytes 10616832 | tf_op jit(solution)/shard_map/all_to_all | solution.py:36
  (16 shorter events, 0.0 us)
Async XLA Ops:
  64.1 12.7 %copy-start = (f32[1152]{0:T(1024)S(1)}, f32[1152]{0:T(1024)}, u32[]{:S(2)}) copy-start(f32[1152]{0:T(1024)} %param.15) | copy-start | bytes 13828
  151.5 65.9 %slice-start.2 = ((s8[5308416]{0:T(1024)(128)(4,1)}), s8[4194304]{0:T(1024)(128)(4,1)S(1)}, s32[]{:S(2)}) async-start(s8[5308416]{0:T(1024)(128)(4,1)} %bitcast.17), calls=%async_computation.5 | async-start | bytes 8388608
  151.5 65.9 %slice-start.3 = ((s8[5308416]{0:T(1024)(128)(4,1)}), s8[1114112]{0:T(1024)(128)(4,1)S(1)}, s32[]{:S(2)}) async-start(s8[5308416]{0:T(1024)(128)(4,1)} %bitcast.17), calls=%async_computation.6 | async-start | bytes 2228224
  217.5 71.1 %copy-start.1 = (f32[288]{0:T(512)S(1)}, f32[288]{0:T(512)}, u32[]{:S(2)}) copy-start(f32[288]{0:T(512)} %param.16) | copy-start | bytes 3460
  217.5 71.1 %copy-start.2 = (f32[288]{0:T(512)S(1)}, f32[288]{0:T(512)}, u32[]{:S(2)}) copy-start(f32[288]{0:T(512)} %param.17) | copy-start | bytes 3460
  281.9 108.4 %all-to-all-start.1 = ((bf16[1152,8,288]{0,2,1:T(8,128)(2,1)}), bf16[1152,8,288]{0,2,1:T(8,128)(2,1)}, u32[]{:S(2)}, u32[]{:S(2)}) async-start(bf16[1152,8,288]{0,2,1:T(8,128)(2,1)} %bitcast.16), calls=%async_computation.1 | async-start | bytes 10616832 | tf_op jit(solution)/shard_map/all_to_all | solution.py:36
  286.6 100.6 %slice-start = ((s8[5308416]{0:T(1024)(128)(4,1)}), s8[1114112]{0:T(1024)(128)(4,1)S(1)}, s32[]{:S(2)}) async-start(s8[5308416]{0:T(1024)(128)(4,1)} %bitcast.13), calls=%async_computation.3 | async-start | bytes 2228224
  381.3 5.9 %slice-start.1 = ((s8[5308416]{0:T(1024)(128)(4,1)}), s8[4194304]{0:T(1024)(128)(4,1)S(1)}, s32[]{:S(2)}) async-start(s8[5308416]{0:T(1024)(128)(4,1)} %bitcast.13), calls=%async_computation.4 | async-start | bytes 8388608
where the time goes:
time: 398 us; the launch traced here: 396 us
  blocking collectives  249 us (63%)
  local copies, waits for them, and re-layouts  93.1 us (23%)
  other arithmetic  49 us (12%)
  starting transfers between devices  4.65 us (1%)
    unnamed x1, blocking collectives  92.5 us
    unnamed x22, local copies, waits for them, and re-layouts  76.4 us
    all_to_all x1, blocking collectives, per_device(): lax.all_to_all(narrow_value, 'rows', split_axis=1, concat_axis=0, tiled=T...  65.9 us
    all_to_all x1, blocking collectives, per_device(): lax.all_to_all(narrow_query, 'rows', split_axis=1, concat_axis=0, tiled=T...  64.5 us
    convert_element_type x1, other arithmetic, per_device(): (whole_value / scale_value).astype(jnp.bfloat16)  27.4 us
    pmax x1, blocking collectives, per_device(): lax.pmax((jnp.max(jnp.abs(whole_query), axis=0), jnp.max(jnp.abs(whole_ke...  25.8 us
    reduce_max x1, other arithmetic, per_device(): jnp.max(jnp.abs(whole_value), axis=0)  21.5 us
  transfers between devices with their start and end apart: 1, of which 0 were waited for; matrix products, arithmetic and copies ran while one was open for 3% of the time, Pallas kernels for 0%

commit v1 on v0

--- a/solution.py
+++ b/solution.py
@@ -2,6 +2,18 @@
 import jax.numpy as jnp
 from jax import lax
 from jax.sharding import PartitionSpec as P
+
+
+def sent_to_each(shard, axis, split, join):
+    ways, here = (lax.axis_size(axis), lax.axis_index(axis))
+    width = shard.shape[split] // ways
+    turned = jnp.roll(shard, -here * width, axis=split)
+    got = [lax.slice_in_dim(turned, 0, width, axis=split)]
+    for far in range(1, ways):
+        sent = lax.slice_in_dim(turned, far * width, (far + 1) * width, axis=split)
+        got.append(lax.ppermute(sent, axis, [(d, (d + far) % ways) for d in range(ways)]))
+    line = jnp.concatenate(got[::-1], axis=join)
+    return jnp.roll(line, (here + 1) * got[0].shape[join], axis=join)
 
 
 def per_device(
@@ -32,7 +44,7 @@
         (whole_value / scale_value).astype(jnp.bfloat16),
     )
     serving_query, serving_key, serving_value = (
-        lax.all_to_all(narrow_query, "rows", split_axis=1, concat_axis=0, tiled=True),
+        sent_to_each(narrow_query, "rows", 1, 0),
         lax.all_to_all(narrow_key, "rows", split_axis=1, concat_axis=0, tiled=True),
         lax.all_to_all(narrow_value, "rows", split_axis=1, concat_axis=0, tiled=True),
     )

time: 398 us -> 397 us (level)
  blocking collectives: 249 us -> 158 us
  waiting for transfers between devices: 0.01 us -> 40 us
  local copies, waits for them, and re-layouts: 93.1 us -> 123 us
  starting transfers between devices: 4.65 us -> 16.7 us
  other arithmetic: 49 us -> 56.9 us
    all_to_all x2 -> x0, blocking collectives: 130 us -> none  [the longest x1 65.9 us: per_device(): lax.all_to_all(narrow_value, 'rows', split_axis=1, concat_axis=0, tiled=T...]
    unnamed x1, blocking collectives: 92.5 us -> 132 us
    all_to_all x0 -> x1, waiting for transfers between devices: none -> 23.8 us  [per_device(): lax.all_to_all(narrow_value, 'rows', split_axis=1, concat_axis=0, tiled=T...]
    unnamed x22 -> x31, local copies, waits for them, and re-layouts: 76.4 us -> 98.2 us
    ppermute x0 -> x7, waiting for transfers between devices: none -> 16.2 us  [sent_to_each(): lax.ppermute(sent, axis, [(d, (d + far) % ways) for d in range(ways)])]
    concatenate x0 -> x1, other arithmetic: none -> 7.97 us  [sent_to_each(): turned = jnp.roll(shard, -here * width, axis=split)]
    dynamic_slice x0 -> x1, local copies, waits for them, and re-layouts: none -> 7.06 us  [sent_to_each(): return jnp.roll(line, (here + 1) * got[0].shape[join], axis=join)]
    ppermute x0 -> x7, starting transfers between devices: none -> 6.99 us  [sent_to_each(): lax.ppermute(sent, axis, [(d, (d + far) % ways) for d in range(ways)])]
  transfers between devices with their start and end apart: 1 -> 9, of which waited for: 0 -> 3; matrix products, arithmetic and copies ran while one was open for 3% -> 12% of each run, Pallas kernels for 0% -> 0%
where the time goes in v1:
time: 397 us; the launch traced here: 395 us
  blocking collectives  158 us (40%)
  local copies, waits for them, and re-layouts  123 us (31%)
  other arithmetic  56.9 us (14%)
  waiting for transfers between devices  40 us (10%)
  starting transfers between devices  16.7 us (4%)
    unnamed x1, blocking collectives  132 us
    unnamed x31, local copies, waits for them, and re-layouts  98.2 us
    convert_element_type x1, other arithmetic, per_device(): (whole_value / scale_value).astype(jnp.bfloat16)  27.4 us
    pmax x1, blocking collectives, per_device(): lax.pmax((jnp.max(jnp.abs(whole_query), axis=0), jnp.max(jnp.abs(whole_ke...  25.8 us
    all_to_all x1, waiting for transfers between devices, per_device(): lax.all_to_all(narrow_value, 'rows', split_axis=1, concat_axis=0, tiled=T...  23.8 us
    reduce_max x1, other arithmetic, per_device(): jnp.max(jnp.abs(whole_value), axis=0)  21.6 us
    ppermute x7, waiting for transfers between devices, sent_to_each(): lax.ppermute(sent, axis, [(d, (d + far) % ways) for d in range(ways)])  16.2 us
    concatenate x1, other arithmetic, sent_to_each(): turned = jnp.roll(shard, -here * width, axis=split)  7.97 us
  transfers between devices with their start and end apart: 9, of which 3 were waited for; matrix products, arithmetic and copies ran while one was open for 12% of the time, Pallas kernels for 0%

profile of v1, /device:TPU:0, one launch (start us, length us, event | category | flops | bytes accessed | tf_op | source)
XLA Modules:
  0.0 394.8 jit_solution(4211357220524366288)
XLA Ops:
  0.6 12.7 %copy.30 = f32[1152,2304]{0,1:T(8,128)} copy(f32[1152,2304]{1,0:T(8,128)} %param.9) | data formatting | bytes 21233664 | tf_op args[0]
  13.3 12.7 %copy.31 = f32[1152,2304]{0,1:T(8,128)} copy(f32[1152,2304]{1,0:T(8,128)} %param.10) | data formatting | bytes 21233664 | tf_op args[1]
  26.0 12.7 %copy.32 = f32[1152,2304]{0,1:T(8,128)} copy(f32[1152,2304]{1,0:T(8,128)} %param.11) | data formatting | bytes 21233664 | tf_op args[2]
  38.7 12.7 %copy.33 = f32[1152,2304]{0,1:T(8,128)} copy(f32[1152,2304]{1,0:T(8,128)} %param.12) | data formatting | bytes 21233664 | tf_op args[3]
  51.4 12.7 %copy.35 = f32[1152,2304]{0,1:T(8,128)} copy(f32[1152,2304]{1,0:T(8,128)} %param.13) | data formatting | bytes 21233664 | tf_op args[4]
  64.0 12.7 %copy.36 = f32[1152,2304]{0,1:T(8,128)} copy(f32[1152,2304]{1,0:T(8,128)} %param.14) | data formatting | bytes 21233664 | tf_op args[5]
  76.7 21.6 %abs_reduce_fusion = (f32[2304]{0:T(1024)S(1)}, f32[2304]{0:T(1024)S(1)}, f32[2304]{0:T(1024)S(1)}) fusion(f32[1152,2304]{0,1:T(8,128)} %copy.36, f32[1152]{0:T(1024)S(1)} %broadcast_subtract_fusion, f32[1152,2304]{0,1:T(8,128)} %copy.35, f32[1152]{0:T(1024)S(1)} %copy-done.1, f32[1152,2304]{0,1:T(8,128)} %copy.33, f32[1152,2304]{0,1:T(8,128)} %copy.32, ...), kind=kLoop, calls=%fused_computation.3 | loop fusion | flops 39806208 | bytes 63737856 | tf_op jit(solution)/shard_map/reduce_max | solution.py:37
  98.3 25.8 %all-reduce.1 = (f32[2304]{0:T(1024)S(1)}, f32[2304]{0:T(1024)S(1)}, f32[2304]{0:T(1024)S(1)}) all-reduce(f32[2304]{0:T(1024)S(1)} %get-tuple-element.9, f32[2304]{0:T(1024)S(1)} %get-tuple-element.8, f32[2304]{0:T(1024)S(1)} %get-tuple-element.7), channel_id=1, replica_groups=mesh['rows'=8,'tp'=4] {'rows'}, use_global_device_ids=true, to_apply=%region_1.0 | all-reduce | flops 6912 | bytes 55296 | tf_op jit(solution)/shard_map/pmax | solution.py:33
  124.1 27.4 %divide_convert_fusion = (bf16[1152,2304]{0,1:T(8,128)(2,1)}, bf16[1152,2304]{0,1:T(8,128)(2,1)}, bf16[1152,2304]{0,1:T(8,128)(2,1)}) fusion(f32[2304]{0:T(1024)S(1)} %get-tuple-element.12, f32[1152,2304]{0,1:T(8,128)} %copy.36, f32[1152]{0:T(1024)S(1)} %broadcast_subtract_fusion, f32[1152,2304]{0,1:T(8,128)} %copy.35, f32[1152]{0:T(1024)S(1)} %copy-done.1, ...), kind=kLoop, calls=%fused_computation.2 | loop fusion | flops 39813120 | bytes 79663104 | tf_op jit(solution)/shard_map/convert_element_type | solution.py:44
  151.5 4.8 %all-to-all-start = ((bf16[1152,8,288]{0,2,1:T(8,128)(2,1)}), bf16[1152,8,288]{0,2,1:T(8,128)(2,1)}, u32[]{:S(2)}, u32[]{:S(2)}) async-start(bf16[1152,8,288]{0,2,1:T(8,128)(2,1)} %bitcast.9), calls=%async_computation | async-start | bytes 10616832 | tf_op jit(solution)/shard_map/all_to_all | solution.py:48
  156.4 8.0 %fusion = bf16[1152,2304]{0,1:T(8,128)(2,1)S(1)} fusion(s32[]{:T(128)S(6)} %select_n.29, bf16[1152,2304]{0,1:T(8,128)(2,1)} %get-tuple-element.21), kind=kLoop, calls=%fused_computation.11 | loop fusion | flops 10616832 | bytes 10616836 | tf_op jit(solution)/shard_map/jit(_roll_dynamic)/concatenate | solution.py:10
  164.4 2.4 copy-done
  166.7 2.2 fusion.1
  168.9 2.4 collective-permute-start
  175.9 131.7 %all-reduce = bf16[9216]{0:T(1024)(128)(2,1)} all-reduce(bf16[9216]{0:T(1024)(128)(2,1)S(1)} %dynamic-update-slice), channel_id=1, replica_groups=mesh['rows'=8,'tp'=4] {'rows','tp'}, use_global_device_ids=true, to_apply=%add | all-reduce | flops 9216 | bytes 36864
  307.6 2.3 collective-permute-start.5
  313.7 4.9 %all-to-all-start.1 = ((bf16[1152,8,288]{0,2,1:T(8,128)(2,1)}), bf16[1152,8,288]{0,2,1:T(8,128)(2,1)}, u32[]{:S(2)}, u32[]{:S(2)}) async-start(bf16[1152,8,288]{0,2,1:T(8,128)(2,1)} %bitcast.8), calls=%async_computation.1 | async-start | bytes 10616832 | tf_op jit(solution)/shard_map/all_to_all | solution.py:49
  319.5 7.2 %collective-permute-done.5 = bf16[1152,288]{0,1:T(8,128)(2,1)} collective-permute-done((bf16[1152,288]{0,1:T(8,128)(2,1)}, bf16[1152,288]{0,1:T(8,128)(2,1)}, u32[]{:S(2)}, u32[]{:S(2)}) %collective-permute-start.5) | collective-permute-done | bytes 663584 | tf_op jit(solution)/shard_map/ppermute | solution.py:14
  328.7 9.0 %collective-permute-done.6 = bf16[1152,288]{0,1:T(8,128)(2,1)} collective-permute-done((bf16[1152,288]{0,1:T(8,128)(2,1)}, bf16[1152,288]{0,1:T(8,128)(2,1)}, u32[]{:S(2)}, u32[]{:S(2)}) %collective-permute-start.6) | collective-permute-done | bytes 663584 | tf_op jit(solution)/shard_map/ppermute | solution.py:14
  339.8 2.0 slice_dynamic-update-slice_fusion
  352.5 7.1 %constant_dynamic-slice_fusion = bf16[9216,288]{0,1:T(8,128)(2,1)} fusion(bf16[18432,288]{0,1:T(8,128)(2,1)} %slice_dynamic-update-slice_fusion.1, s32[]{:T(128)S(6)} %select_n.31), kind=kLoop, calls=%fused_computation.30 | loop fusion | bytes 10616836 | tf_op jit(solution)/shard_map/jit(_roll_dynamic)/dynamic_slice | solution.py:16
  359.6 5.7 %copy.38 = bf16[8,36,8,1152]{3,2,0,1:T(8,128)(2,1)} copy(bf16[8,36,8,1152]{3,2,1,0:T(8,128)(2,1)} %bitcast.4) | data formatting | bytes 10616832 | tf_op jit(solution)/shard_map/all_to_all | solution.py:48
  365.3 23.8 %all-to-all-done.1 = bf16[1152,8,288]{0,2,1:T(8,128)(2,1)} async-done(((bf16[1152,8,288]{0,2,1:T(8,128)(2,1)}), bf16[1152,8,288]{0,2,1:T(8,128)(2,1)}, u32[]{:S(2)}, u32[]{:S(2)}) %all-to-all-start.1) | async-done | bytes 5308448 | tf_op jit(solution)/shard_map/all_to_all | solution.py:49
  389.1 5.7 %copy.39 = bf16[8,36,8,1152]{3,2,0,1:T(8,128)(2,1)} copy(bf16[8,36,8,1152]{3,2,1,0:T(8,128)(2,1)} %bitcast.6) | data formatting | bytes 10616832 | tf_op jit(solution)/shard_map/all_to_all | solution.py:49
  (40 shorter events, 24.1 us)
Async XLA Ops:
  64.0 12.7 %copy-start.1 = (f32[1152]{0:T(1024)S(1)}, f32[1152]{0:T(1024)}, u32[]{:S(2)}) copy-start(f32[1152]{0:T(1024)} %param.15) | copy-start | bytes 13828
  151.5 162.2 %all-to-all-start = ((bf16[1152,8,288]{0,2,1:T(8,128)(2,1)}), bf16[1152,8,288]{0,2,1:T(8,128)(2,1)}, u32[]{:S(2)}, u32[]{:S(2)}) async-start(bf16[1152,8,288]{0,2,1:T(8,128)(2,1)} %bitcast.9), calls=%async_computation | async-start | bytes 10616832 | tf_op jit(solution)/shard_map/all_to_all | solution.py:48
  156.3 19.3 %copy-start.2 = (f32[288]{0:T(512)S(1)}, f32[288]{0:T(512)}, u32[]{:S(2)}) copy-start(f32[288]{0:T(512)} %param.16) | copy-start | bytes 3460
  156.3 19.3 %copy-start.3 = (f32[288]{0:T(512)S(1)}, f32[288]{0:T(512)}, u32[]{:S(2)}) copy-start(f32[288]{0:T(512)} %param.17) | copy-start | bytes 3460
  164.3 2.4 copy-start
  168.9 138.7 %collective-permute-start = (bf16[1152,288]{0,1:T(8,128)(2,1)}, bf16[1152,288]{0,1:T(8,128)(2,1)S(1)}, u32[]{:S(2)}, u32[]{:S(2)}) collective-permute-start(bf16[1152,288]{0,1:T(8,128)(2,1)} %get-tuple-element.19), channel_id=1, source_target_pairs={{0,28},{4,0},{8,4},{12,8},{16,12},{20,16},{24,20},{28,24},{1,29},{... | collective-permute-start | bytes 1990664 | tf_op jit(solution)/shard_map/ppermute | solution.py:14
  171.3 139.5 %collective-permute-start.1 = (bf16[1152,288]{0,1:T(8,128)(2,1)}, bf16[1152,288]{0,1:T(8,128)(2,1)S(1)}, u32[]{:S(2)}, u32[]{:S(2)}) collective-permute-start(bf16[1152,288]{0,1:T(8,128)(2,1)} %get-tuple-element.18), channel_id=1, source_target_pairs={{0,24},{4,28},{8,0},{12,4},{16,8},{20,12},{24,16},{28,20},{1,25},{... | collective-permute-start | bytes 1990664 | tf_op jit(solution)/shard_map/ppermute | solution.py:14
  171.9 139.9 %collective-permute-start.2 = (bf16[1152,288]{0,1:T(8,128)(2,1)}, bf16[1152,288]{0,1:T(8,128)(2,1)S(1)}, u32[]{:S(2)}, u32[]{:S(2)}) collective-permute-start(bf16[1152,288]{0,1:T(8,128)(2,1)} %get-tuple-element.17), channel_id=1, source_target_pairs={{0,20},{4,24},{8,28},{12,0},{16,4},{20,8},{24,12},{28,16},{1,21},{... | collective-permute-start | bytes 1990664 | tf_op jit(solution)/shard_map/ppermute | solution.py:14
  172.0 140.8 %collective-permute-start.3 = (bf16[1152,288]{0,1:T(8,128)(2,1)}, bf16[1152,288]{0,1:T(8,128)(2,1)S(1)}, u32[]{:S(2)}, u32[]{:S(2)}) collective-permute-start(bf16[1152,288]{0,1:T(8,128)(2,1)} %get-tuple-element.16), channel_id=1, source_target_pairs={{0,16},{4,20},{8,24},{12,28},{16,0},{20,4},{24,8},{28,12},{1,17},{... | collective-permute-start | bytes 1990664 | tf_op jit(solution)/shard_map/ppermute | solution.py:14
  173.4 145.1 %collective-permute-start.4 = (bf16[1152,288]{0,1:T(8,128)(2,1)}, bf16[1152,288]{0,1:T(8,128)(2,1)S(1)}, u32[]{:S(2)}, u32[]{:S(2)}) collective-permute-start(bf16[1152,288]{0,1:T(8,128)(2,1)} %get-tuple-element.15), channel_id=1, source_target_pairs={{0,12},{4,16},{8,20},{12,24},{16,28},{20,0},{24,4},{28,8},{1,13},{... | collective-permute-start | bytes 1990664 | tf_op jit(solution)/shard_map/ppermute | solution.py:14
  307.6 19.1 %collective-permute-start.5 = (bf16[1152,288]{0,1:T(8,128)(2,1)}, bf16[1152,288]{0,1:T(8,128)(2,1)}, u32[]{:S(2)}, u32[]{:S(2)}) collective-permute-start(bf16[1152,288]{0,1:T(8,128)(2,1)} %get-tuple-element.14), channel_id=1, source_target_pairs={{0,8},{4,12},{8,16},{12,20},{16,24},{20,28},{24,0},{28,4},{1,9},{5... | collective-permute-start | bytes 1990664 | tf_op jit(solution)/shard_map/ppermute | solution.py:14
  310.8 26.9 %collective-permute-start.6 = (bf16[1152,288]{0,1:T(8,128)(2,1)}, bf16[1152,288]{0,1:T(8,128)(2,1)}, u32[]{:S(2)}, u32[]{:S(2)}) collective-permute-start(bf16[1152,288]{0,1:T(8,128)(2,1)} %get-tuple-element.13), channel_id=1, source_target_pairs={{0,4},{4,8},{8,12},{12,16},{16,20},{20,24},{24,28},{28,0},{1,5},{5... | collective-permute-start | bytes 1990664 | tf_op jit(solution)/shard_map/ppermute | solution.py:14
  313.7 75.5 %all-to-all-start.1 = ((bf16[1152,8,288]{0,2,1:T(8,128)(2,1)}), bf16[1152,8,288]{0,2,1:T(8,128)(2,1)}, u32[]{:S(2)}, u32[]{:S(2)}) async-start(bf16[1152,8,288]{0,2,1:T(8,128)(2,1)} %bitcast.8), calls=%async_computation.1 | async-start | bytes 10616832 | tf_op jit(solution)/shard_map/all_to_all | solution.py:49
